TPU v7x, 32 devices: a whole 2x2x4 slice. The times are simulated.
32 devices in a mesh: seq: 16 (over z, y, core), head: 2 (over x).
Axes of the slice: x: 2, y: 2, z: 4, core: 2. Of those that a mesh axis runs over, the one named last changes fastest.
Arguments:
- tokens: bfloat16 [16384, 768], P(('seq', 'head')), may hold values from -6 to 6
- w_query: bfloat16 [768, 768], replicated, may hold values from -0.3125 to 0.3125
- w_key: bfloat16 [768, 768], replicated, may hold values from -0.21875 to 0.21875
- w_value: bfloat16 [768, 768], replicated, may hold values from -0.21875 to 0.21875
- w_out: bfloat16 [768, 768], replicated, may hold values from -3.5 to 3.5
- gain_attn: float32 [768], replicated, may hold values from 0.5 to 1.5
- shift_attn: float32 [768], replicated, may hold values from -3 to 3
- w_up: bfloat16 [768, 3072], replicated, may hold values from -0.21875 to 0.21875
- w_down: bfloat16 [3072, 768], replicated, may hold values from -0.109375 to 0.109375
- gain_mlp: float32 [768], replicated, may hold values from 0.5 to 1.5
- shift_mlp: float32 [768], replicated, may hold values from -3 to 3
- cotangent: bfloat16 [16384, 768], P(('seq', 'head')), may hold values from -6 to 6
- lengths: int32 [8], replicated, may hold values from 1 to 64, 256 in all
- seq_order: int32 [8], replicated, may hold values from 0 to 7, each once
- rand_blocks: int32 [256, 3], P('seq'), may hold values from 0 to 65535
Outputs:
- output: bfloat16 [16384, 768], P(('seq', 'head'))
- grad_tokens: float32 [16384, 768], P(('seq', 'head'))
- grad_w_query: float32 [768, 768], P('seq')
- grad_w_key: float32 [768, 768], P('seq')
- grad_w_value: float32 [768, 768], P('seq')
- grad_w_out: float32 [768, 768], P('seq')
- grad_gain_attn: float32 [768], P('seq')
- grad_shift_attn: float32 [768], P('seq')
- grad_w_up: float32 [768, 3072], P('seq')
- grad_w_down: float32 [3072, 768], P('seq')
- grad_gain_mlp: float32 [768], P('seq')
- grad_shift_mlp: float32 [768], P('seq')
Inputs may be any that keep to these rules, and one draw needn't show every extreme that they name: lengths of the 8 sequences in blocks of 64 tokens; they sum to 256 and the longest is exactly 64. `seq_order`: each of 0 to 7 once.
All inputs are finite; a program needn't handle non-finite values.
Results may differ from a plain program's by a relative error of at most 0.017.
Values may be sent and summed in bfloat16 or wider, within the bound.
A program may use at most 320 MiB of HBM per device.

v0:
```python
import jax
import jax.numpy as jnp
from jax import lax
from jax.sharding import PartitionSpec as P

DH = 64
BLK = 64
MAXB = 64
eps_norm = 1e-06


def shifted(value, axis, steps):
    count = lax.axis_size(axis)
    first, last = (max(0, -steps), min(count, count - steps))
    return lax.ppermute(value, axis, [(source, source + steps) for source in range(first, last)])


def block_slots(blocks, rand_rows, lengths, seq_order):
    seq_count = lengths.shape[0]
    seq_ids = jnp.arange(seq_count, dtype=jnp.int32)
    packed = jnp.sum(jnp.where(seq_order[:, None] == seq_ids[None, :], lengths[None, :], 0), axis=1)
    seq_ends = jnp.cumsum(packed)
    starts = seq_ends - packed
    holder = jnp.sum((seq_ends[None, :] <= blocks[:, None]).astype(jnp.int32), axis=1)
    chosen = holder[:, None] == seq_ids[None, :]
    seq_first = jnp.sum(jnp.where(chosen, starts[None, :], 0), axis=1)
    seq_span = jnp.sum(jnp.where(chosen, packed[None, :], 0), axis=1)
    offset = blocks - seq_first
    rand_pos = seq_first[:, None] + jnp.mod(rand_rows, seq_span[:, None])
    fixed_cand = jnp.stack(
        [blocks - 1, blocks, blocks + 1, seq_first, seq_first + seq_span - 1], axis=1
    )
    candidate = jnp.concatenate([fixed_cand, rand_pos], axis=1)
    fixed_live = jnp.stack(
        [offset > 0, offset >= 0, offset < seq_span - 1, offset >= 0, offset >= 0], axis=1
    )
    usable = jnp.concatenate([fixed_live, rand_pos >= 0], axis=1)
    kept_list = []
    for column in range(candidate.shape[1]):
        unique = usable[:, column]
        for earlier in range(column):
            unique = unique & jnp.logical_not(
                kept_list[earlier] & (candidate[:, earlier] == candidate[:, column])
            )
        kept_list.append(unique)
    is_live = jnp.stack(kept_list, axis=1)
    key_blocks = jnp.where(is_live, candidate, blocks[:, None])
    return (key_blocks, is_live)


def norm_forward(values, gain_vec, shift_vec):
    center = values - jnp.mean(values, axis=-1, keepdims=True)
    spread = jnp.mean(center * center, axis=-1, keepdims=True)
    inv_dev = lax.rsqrt(spread + eps_norm)
    x_hat = center * inv_dev
    return (x_hat * gain_vec + shift_vec, x_hat, inv_dev)


def norm_backward(grad_in, x_hat, inv_dev, gain_vec):
    grad_gain = jnp.sum(grad_in * x_hat, axis=0)
    grad_shift = jnp.sum(grad_in, axis=0)
    grad_hat = grad_in * gain_vec
    grad_mean = jnp.mean(grad_hat, axis=-1, keepdims=True)
    grad_proj = jnp.mean(grad_hat * x_hat, axis=-1, keepdims=True)
    return (inv_dev * (grad_hat - grad_mean - x_hat * grad_proj), grad_gain, grad_shift)


def gelu_tanh(values):
    return jax.nn.gelu(values, approximate=True)


def kv_from_below(piece):
    return shifted(piece, "seq", 1)


def kv_from_above(piece):
    return shifted(piece, "seq", -1)


def kv_again_below(piece):
    return shifted(piece, "seq", 1)


def kv_again_above(piece):
    return shifted(piece, "seq", -1)


def fill_cycle(kv_local, cycle_reach, from_below, from_above):
    slot_total = 2 * cycle_reach + 1
    buffer = jnp.zeros((slot_total,) + kv_local.shape, kv_local.dtype)
    buffer = lax.dynamic_update_index_in_dim(buffer, kv_local, cycle_reach, 0)

    def advance(cycle_step, cycle_state):
        below_piece, above_piece, filled = cycle_state
        below_piece = from_below(below_piece)
        above_piece = from_above(above_piece)
        filled = lax.dynamic_update_index_in_dim(
            filled, below_piece, cycle_reach - cycle_step - 1, 0
        )
        filled = lax.dynamic_update_index_in_dim(
            filled, above_piece, cycle_reach + cycle_step + 1, 0
        )
        return (below_piece, above_piece, filled)

    return lax.fori_loop(0, cycle_reach, advance, (kv_local, kv_local, buffer))[2]


def gather_slots(buffer, local_rows, heads_here):
    flat_rows = buffer.reshape(-1, BLK, buffer.shape[-1])
    picked = flat_rows[local_rows]
    split_shape = picked.shape[:3] + (2, heads_here, DH)
    picked = picked.reshape(split_shape)
    return (picked[:, :, :, 0], picked[:, :, :, 1])


def score_blocks(q_blocks, key_rows, is_live, score_scale):
    scores = (
        jnp.einsum("cqhd,cskhd->chqsk", q_blocks, key_rows, preferred_element_type=jnp.float32)
        * score_scale
    )
    scores = jnp.where(is_live[:, None, None, :, None], scores, -1e30)
    return scores.reshape(scores.shape[0], scores.shape[1], scores.shape[2], -1)


def body(
    tokens,
    w_query,
    w_key,
    w_value,
    w_out,
    gain_attn,
    shift_attn,
    w_up,
    w_down,
    gain_mlp,
    shift_mlp,
    cotangent,
    lengths,
    seq_order,
    rand_blocks,
):
    score_scale = DH ** (-0.5)
    queries = jnp.dot(tokens, w_query, preferred_element_type=jnp.float32).astype(jnp.bfloat16)
    key_proj = jnp.dot(tokens, w_key, preferred_element_type=jnp.float32).astype(jnp.bfloat16)
    value_proj = jnp.dot(tokens, w_value, preferred_element_type=jnp.float32).astype(jnp.bfloat16)
    q_local, k_local, v_local = (
        lax.all_to_all(queries, "head", split_axis=1, concat_axis=0, tiled=True),
        lax.all_to_all(key_proj, "head", split_axis=1, concat_axis=0, tiled=True),
        lax.all_to_all(value_proj, "head", split_axis=1, concat_axis=0, tiled=True),
    )
    stretch_rows = q_local.shape[0]
    heads_here = q_local.shape[1] // DH
    stretch_blocks = stretch_rows // BLK
    cycle_reach = MAXB * BLK // stretch_rows
    kv_local = jnp.concatenate([k_local, v_local], axis=1)
    buffer = fill_cycle(kv_local, cycle_reach, kv_from_below, kv_from_above)
    seq_index = lax.axis_index("seq")
    blocks = seq_index * stretch_blocks + jnp.arange(stretch_blocks, dtype=jnp.int32)
    key_blocks, is_live = block_slots(blocks, rand_blocks, lengths, seq_order)
    local_rows = key_blocks - (seq_index - cycle_reach) * stretch_blocks
    slot_count = key_blocks.shape[1]
    q_blocks = q_local.reshape(stretch_blocks, BLK, heads_here, DH)
    key_rows, value_rows = gather_slots(buffer, local_rows, heads_here)
    scores = score_blocks(q_blocks, key_rows, is_live, score_scale)
    row_max = jnp.max(scores, axis=-1, keepdims=True)
    exp_scores = jnp.exp(scores - row_max)
    row_total = jnp.sum(exp_scores, axis=-1, keepdims=True)
    attn_probs = exp_scores / row_total
    log_total = row_max + jnp.log(row_total)
    five_shape = (stretch_blocks, heads_here, BLK, slot_count, BLK)
    weights = attn_probs.astype(jnp.bfloat16).reshape(five_shape)
    context = jnp.einsum(
        "chqsk,cskhd->cqhd", weights, value_rows, preferred_element_type=jnp.float32
    )
    context = context.astype(jnp.bfloat16).reshape(stretch_rows, -1)
    context_tok = lax.all_to_all(context, "head", split_axis=0, concat_axis=1, tiled=True)
    attn_out = jnp.dot(context_tok, w_out, preferred_element_type=jnp.float32)
    normed, hat_one, dev_one = norm_forward(
        tokens.astype(jnp.float32) + attn_out, gain_attn, shift_attn
    )
    normed_low = normed.astype(jnp.bfloat16)
    hidden_pre = jnp.dot(normed_low, w_up, preferred_element_type=jnp.float32)
    hidden = gelu_tanh(hidden_pre).astype(jnp.bfloat16)
    mlp_out = jnp.dot(hidden, w_down, preferred_element_type=jnp.float32)
    output, hat_two, dev_two = norm_forward(normed + mlp_out, gain_mlp, shift_mlp)
    grad_two, grad_gain_mlp, grad_shift_mlp = norm_backward(
        cotangent.astype(jnp.float32), hat_two, dev_two, gain_mlp
    )
    grad_mlp = grad_two.astype(jnp.bfloat16)
    grad_w_down = jnp.dot(hidden.T, grad_mlp, preferred_element_type=jnp.float32)
    grad_hidden = jnp.dot(grad_mlp, w_down.T, preferred_element_type=jnp.float32)
    gelu_out, gelu_pull = jax.vjp(gelu_tanh, hidden_pre)
    grad_pre = gelu_pull(grad_hidden)[0].astype(jnp.bfloat16)
    grad_w_up = jnp.dot(normed_low.T, grad_pre, preferred_element_type=jnp.float32)
    grad_normed = grad_two + jnp.dot(grad_pre, w_up.T, preferred_element_type=jnp.float32)
    grad_one, grad_gain_attn, grad_shift_attn = norm_backward(
        grad_normed, hat_one, dev_one, gain_attn
    )
    grad_attn = grad_one.astype(jnp.bfloat16)
    grad_w_out = jnp.dot(context_tok.T, grad_attn, preferred_element_type=jnp.float32)
    grad_context = jnp.dot(grad_attn, w_out.T, preferred_element_type=jnp.float32).astype(
        jnp.bfloat16
    )
    grad_ctx_local = lax.all_to_all(grad_context, "head", split_axis=1, concat_axis=0, tiled=True)
    buffer_back = fill_cycle(kv_local, cycle_reach, kv_again_below, kv_again_above)
    key_again, value_again = gather_slots(buffer_back, local_rows, heads_here)
    scores_again = score_blocks(q_blocks, key_again, is_live, score_scale)
    probs_again = jnp.exp(scores_again - log_total)
    weights_again = probs_again.astype(jnp.bfloat16).reshape(five_shape)
    grad_blocks = grad_ctx_local.reshape(stretch_blocks, BLK, heads_here, DH)
    grad_probs = jnp.einsum(
        "cqhd,cskhd->chqsk", grad_blocks, value_again, preferred_element_type=jnp.float32
    )
    grad_probs = grad_probs.reshape(probs_again.shape)
    grad_value_rows = jnp.einsum(
        "chqsk,cqhd->cskhd", weights_again, grad_blocks, preferred_element_type=jnp.float32
    )
    row_inner = jnp.sum(probs_again * grad_probs, axis=-1, keepdims=True)
    grad_scores = (probs_again * (grad_probs - row_inner)).astype(jnp.bfloat16).reshape(five_shape)
    grad_query = (
        jnp.einsum("chqsk,cskhd->cqhd", grad_scores, key_again, preferred_element_type=jnp.float32)
        * score_scale
    )
    grad_key_rows = (
        jnp.einsum("chqsk,cqhd->cskhd", grad_scores, q_blocks, preferred_element_type=jnp.float32)
        * score_scale
    )
    slot_grads = jnp.concatenate(
        [
            grad_key_rows.reshape(stretch_blocks, slot_count, BLK, -1),
            grad_value_rows.reshape(stretch_blocks, slot_count, BLK, -1),
        ],
        axis=-1,
    )
    width_kv = slot_grads.shape[-1]
    grad_buffer = jnp.zeros((buffer.shape[0] * stretch_blocks, BLK, width_kv), jnp.float32)
    grad_buffer = grad_buffer.at[local_rows.reshape(-1)].add(slot_grads.reshape(-1, BLK, width_kv))
    grad_buffer = grad_buffer.reshape(buffer.shape[0], stretch_rows, width_kv)

    def carry_back(cycle_step, cycle_state):
        below_acc, above_acc = cycle_state
        below_term = lax.dynamic_index_in_dim(grad_buffer, cycle_step, 0, keepdims=False)
        above_term = lax.dynamic_index_in_dim(
            grad_buffer, 2 * cycle_reach - cycle_step, 0, keepdims=False
        )
        below_acc = shifted((below_acc + below_term).astype(jnp.bfloat16), "seq", -1).astype(
            jnp.float32
        )
        above_acc = shifted((above_acc + above_term).astype(jnp.bfloat16), "seq", 1).astype(
            jnp.float32
        )
        return (below_acc, above_acc)

    zero_rows = jnp.zeros((stretch_rows, width_kv), jnp.float32)
    below_acc, above_acc = lax.fori_loop(0, cycle_reach, carry_back, (zero_rows, zero_rows))
    grad_kv = below_acc + above_acc + grad_buffer[cycle_reach]
    half_width = width_kv // 2
    grad_key_local = grad_kv[:, :half_width].astype(jnp.bfloat16)
    grad_value_local = grad_kv[:, half_width:].astype(jnp.bfloat16)
    grad_query_local = grad_query.reshape(stretch_rows, -1).astype(jnp.bfloat16)
    grad_q_tok, grad_k_tok, grad_v_tok = (
        lax.all_to_all(grad_query_local, "head", split_axis=0, concat_axis=1, tiled=True),
        lax.all_to_all(grad_key_local, "head", split_axis=0, concat_axis=1, tiled=True),
        lax.all_to_all(grad_value_local, "head", split_axis=0, concat_axis=1, tiled=True),
    )
    grad_w_query = jnp.dot(tokens.T, grad_q_tok, preferred_element_type=jnp.float32)
    grad_w_key = jnp.dot(tokens.T, grad_k_tok, preferred_element_type=jnp.float32)
    grad_w_value = jnp.dot(tokens.T, grad_v_tok, preferred_element_type=jnp.float32)
    grad_tokens = grad_one + jnp.dot(grad_q_tok, w_query.T, preferred_element_type=jnp.float32)
    grad_tokens = grad_tokens + jnp.dot(grad_k_tok, w_key.T, preferred_element_type=jnp.float32)
    grad_tokens = grad_tokens + jnp.dot(grad_v_tok, w_value.T, preferred_element_type=jnp.float32)
    grad_terms = (
        grad_w_query,
        grad_w_key,
        grad_w_value,
        grad_w_out,
        grad_gain_attn,
        grad_shift_attn,
        grad_w_up,
        grad_w_down,
        grad_gain_mlp,
        grad_shift_mlp,
    )
    shares = (
        lax.psum_scatter(grad_terms[0], "seq", scatter_dimension=0, tiled=True),
        lax.psum_scatter(grad_terms[1], "seq", scatter_dimension=0, tiled=True),
        lax.psum_scatter(grad_terms[2], "seq", scatter_dimension=0, tiled=True),
        lax.psum_scatter(grad_terms[3], "seq", scatter_dimension=0, tiled=True),
        lax.psum_scatter(grad_terms[4], "seq", scatter_dimension=0, tiled=True),
        lax.psum_scatter(grad_terms[5], "seq", scatter_dimension=0, tiled=True),
        lax.psum_scatter(grad_terms[6], "seq", scatter_dimension=0, tiled=True),
        lax.psum_scatter(grad_terms[7], "seq", scatter_dimension=0, tiled=True),
        lax.psum_scatter(grad_terms[8], "seq", scatter_dimension=0, tiled=True),
        lax.psum_scatter(grad_terms[9], "seq", scatter_dimension=0, tiled=True),
    )
    totals = (
        lax.psum(shares[0].astype(jnp.bfloat16), "head").astype(jnp.float32),
        lax.psum(shares[1].astype(jnp.bfloat16), "head").astype(jnp.float32),
        lax.psum(shares[2].astype(jnp.bfloat16), "head").astype(jnp.float32),
        lax.psum(shares[3].astype(jnp.bfloat16), "head").astype(jnp.float32),
        lax.psum(shares[4].astype(jnp.bfloat16), "head").astype(jnp.float32),
        lax.psum(shares[5].astype(jnp.bfloat16), "head").astype(jnp.float32),
        lax.psum(shares[6].astype(jnp.bfloat16), "head").astype(jnp.float32),
        lax.psum(shares[7].astype(jnp.bfloat16), "head").astype(jnp.float32),
        lax.psum(shares[8].astype(jnp.bfloat16), "head").astype(jnp.float32),
        lax.psum(shares[9].astype(jnp.bfloat16), "head").astype(jnp.float32),
    )
    return (
        output.astype(jnp.bfloat16),
        grad_tokens,
        totals[0],
        totals[1],
        totals[2],
        totals[3],
        totals[4],
        totals[5],
        totals[6],
        totals[7],
        totals[8],
        totals[9],
    )


def solution(mesh):
    return jax.shard_map(
        body,
        mesh=mesh,
        in_specs=(
            P(("seq", "head"), None),
            P(),
            P(),
            P(),
            P(),
            P(),
            P(),
            P(),
            P(),
            P(),
            P(),
            P(("seq", "head"), None),
            P(),
            P(),
            P("seq", None),
        ),
        out_specs=(
            P(("seq", "head"), None),
            P(("seq", "head"), None),
            P("seq", None),
            P("seq", None),
            P("seq", None),
            P("seq", None),
            P("seq"),
            P("seq"),
            P("seq", None),
            P("seq", None),
            P("seq"),
            P("seq"),
        ),
        check_vma=False,
    )
```

profile of v0, /device:TPU:0, one launch (start us, length us, event | category | flops | bytes accessed | tf_op | source)
XLA Modules:
  0.0 1420.9 jit_solution(9601776251737171842)
XLA Ops:
  34.3 6.3 all-to-all-done.1
  48.9 5.9 dynamic_update_slice.22
  54.8 138.4 %while.42 = (s32[]{:T(128)}, bf16[1024,768]{1,0:T(8,128)(2,1)}, bf16[1024,768]{1,0:T(8,128)(2,1)}, bf16[9,1024,768]{2,1,0:T(8,128)(2,1)}, s32[]{:T(128)}, /*inde...) while((s32[]{:T(128)}, bf16[1024,768]{1,0:T(8,128)(2,1)}, bf16[1024,768]{1,0:T(8,128)(2,1)}, ...), condition=%wide.region_1.2_spmd, body=%wide.region_0.1_spmd.sunk | while | flops 10 | bytes 25166100 | solution.py:105
  70.0 32.5 %collective-permute-start = (bf16[1024,768]{1,0:T(8,128)(2,1)}, bf16[1024,768]{1,0:T(8,128)(2,1)S(1)}, u32[]{:S(2)}, u32[]{:S(2)}) collective-permute-start(bf16[1024,768]{1,0:T(8,128)(2,1)} %get-tuple-element.438), channel_id=1, source_target_pairs={{0,2},{2,4},{4,6},{6,8},{8,10},{10,12},{12,14},{14,16},{16,18},{18... | collective-permute-start | bytes 4718600 | tf_op jit(solution)/shard_map/while/body/eval_jaxpr/ppermute | solution.py:15
  116.6 18.9 %collective-permute-start = (bf16[1024,768]{1,0:T(8,128)(2,1)}, bf16[1024,768]{1,0:T(8,128)(2,1)S(1)}, u32[]{:S(2)}, u32[]{:S(2)}) collective-permute-start(bf16[1024,768]{1,0:T(8,128)(2,1)} %get-tuple-element.438), channel_id=1, source_target_pairs={{0,2},{2,4},{4,6},{6,8},{8,10},{10,12},{12,14},{14,16},{16,18},{18... | collective-permute-start | bytes 4718600 | tf_op jit(solution)/shard_map/while/body/eval_jaxpr/ppermute | solution.py:15
  147.8 33.1 %collective-permute-start = (bf16[1024,768]{1,0:T(8,128)(2,1)}, bf16[1024,768]{1,0:T(8,128)(2,1)S(1)}, u32[]{:S(2)}, u32[]{:S(2)}) collective-permute-start(bf16[1024,768]{1,0:T(8,128)(2,1)} %get-tuple-element.438), channel_id=1, source_target_pairs={{0,2},{2,4},{4,6},{6,8},{8,10},{10,12},{12,14},{14,16},{16,18},{18... | collective-permute-start | bytes 4718600 | tf_op jit(solution)/shard_map/while/body/eval_jaxpr/ppermute | solution.py:15
  193.2 13.2 gather_fusion
  206.5 38.9 %reshape.689 = bf16[16,8,64,2,6,64]{5,4,3,2,1,0:T(8,128)(2,1)} reshape(bf16[128,64,768]{2,1,0:T(8,128)(2,1)} %gather_fusion) | data formatting | bytes 25165824 | tf_op jit(solution)/shard_map/reshape | solution.py:112
  245.4 28.4 %slice_bitcast_fusion = (bf16[16,8,64,6,64]{4,3,2,1,0:T(8,128)(2,1)}, bf16[16,8,64,1,6,64]{5,4,3,2,1,0:T(8,128)(2,1)}, bf16[16,8,64,1,6,64]{5,4,3,2,1,0:T(8,128)(2,1)}) fusion(bf16[16,8,64,2,6,64]{5,4,3,2,1,0:T(8,128)(2,1)} %reshape.689), kind=kLoop, calls=%fused_computation.149 | loop fusion | bytes 31457280 | tf_op jit(solution)/shard_map/squeeze | solution.py:113
  273.8 11.3 copy.222
  288.0 22.2 %copy.221 = bf16[16,8,64,1,6,64]{2,5,1,4,0,3:T(8,128)(2,1)} copy(bf16[16,8,64,1,6,64]{5,4,3,2,1,0:T(8,128)(2,1)} %get-tuple-element.343) | data formatting | bytes 12582912
  310.2 13.3 fusion.11
  323.5 11.9 fusion.2
  335.4 16.8 %fusion.44 = bf16[16,64,6,64]{1,3,2,0:T(8,128)(2,1)S(1)} fusion(f32[16,6,64]{2,1,0:T(8,128)S(1)} %fusion.2, f32[16,6,64]{2,1,0:T(8,128)S(1)} %get-tuple-element.360, f32[16,6,64,8,64]{2,4,3,1,0:T(8,128)} %bitcast.270, pred[16,8]{1,0:T(8,128)(4,1)S(1)} %copy.170, bf16[16,8,64,1,6,64]{2,5,1,4,0,3:T(8,128)(2,1)} %copy.221), kind=kOutput, calls=%fused_computation.71 | convolution fusion | flops 418775040 | bytes 19710080 | tf_op jit(solution)/shard_map/chqsk,cskhd->cqhd/dot_general | solution.py:172
  361.2 7.2 all-to-all-done.3
  369.7 5.4 fusion.72
  381.8 8.1 fusion.21
  402.0 11.5 copy.181
  417.6 24.2 %multiply_reduce_fusion = (f32[16,6,64]{2,1,0:T(8,128)S(1)}, f32[16,6,64,512]{2,3,1,0}) fusion(f32[16,6,64]{2,1,0:T(8,128)S(1)} %log_add_fusion, pred[16,8]{1,0:T(8,128)(4,1)S(1)} %copy.170, f32[16,6,64,512]{2,3,1,0} %get-tuple-element.361, bf16[16,6,64,512]{2,3,1,0:T(8,128)(2,1)} %bitcast.275, bf16[16,64,6,64]{1,0,3,2:T(8,128)(2,1)S(1)} %reshape.691), kind=kOutput, calls=%fused_computation.11 | convolution fusion | flops 418375680 | bytes 32292992
  441.7 21.7 %multiply_convert_fusion = bf16[16,6,64,8,64]{2,4,3,1,0:T(8,128)(2,1)} fusion(f32[16,6,64]{2,1,0:T(8,128)S(1)} %get-tuple-element.367, f32[16,6,64]{2,1,0:T(8,128)S(1)} %log_add_fusion, pred[16,8]{1,0:T(8,128)(4,1)S(1)} %copy.170, f32[16,6,64,512]{2,3,1,0} %get-tuple-element.368, f32[16,6,64,512]{2,3,1,0} %get-tuple-element.361), kind=kLoop, calls=%fused_computation.10 | loop fusion | flops 18874368 | bytes 31506560 | tf_op jit(solution)/shard_map/convert_element_type | solution.py:219
  463.4 10.7 fusion.41
  484.0 25.2 %fusion.12 = f32[16,8,64,6,64]{2,4,1,3,0:T(8,128)} fusion(f32[16,6,64]{2,1,0:T(8,128)S(1)} %log_add_fusion, f32[16,6,64,8,64]{2,4,3,1,0:T(8,128)} %bitcast.271, pred[16,8]{1,0:T(8,128)(4,1)S(1)} %copy.170, bf16[16,64,6,64,1]{1,0,3,2,4:T(8,128)(2,1)S(1)} %bitcast.277), kind=kOutput, calls=%fused_computation.27 | convolution fusion | flops 415236096 | bytes 25976960 | tf_op jit(solution)/shard_map/chqsk,cqhd->cskhd/dot_general | solution.py:215
  509.1 13.0 multiply_bitcast_fusion
  522.1 29.1 %copy.190 = f32[16,8,64,6,64]{4,3,2,1,0:T(8,128)} copy(f32[16,8,64,6,64]{4,2,1,3,0:T(8,128)} %multiply_bitcast_fusion) | data formatting | bytes 25165824 | tf_op jit(solution)/shard_map/mul | solution.py:225
  551.2 25.1 %concatenate.51 = f32[128,64,384]{2,1,0:T(8,128)} reshape(f32[16,8,64,6,64]{4,3,2,1,0:T(8,128)} %copy.190) | data formatting | bytes 25165824 | tf_op jit(solution)/shard_map/concatenate | solution.py:228
  576.3 28.8 %copy.193 = f32[16,8,64,6,64]{4,3,2,1,0:T(8,128)} copy(f32[16,8,64,6,64]{2,4,1,3,0:T(8,128)} %fusion.12) | data formatting | bytes 25165824 | tf_op jit(solution)/shard_map/chqsk,cqhd->cskhd/transpose | solution.py:215
  605.1 25.2 %concatenate.52 = f32[128,64,384]{2,1,0:T(8,128)} reshape(f32[16,8,64,6,64]{4,3,2,1,0:T(8,128)} %copy.193) | data formatting | bytes 25165824 | tf_op jit(solution)/shard_map/concatenate | solution.py:228
  635.1 17.4 %pad_maximum_fusion = f32[128,64,768]{2,1,0:T(8,128)} fusion(f32[128,64,384]{2,1,0:T(8,128)} %concatenate.52, f32[128,64,384]{2,1,0:T(8,128)} %concatenate.51), kind=kLoop, calls=%fused_computation.8 | loop fusion | flops 6291456 | bytes 50331648 | tf_op jit(solution)/shard_map/concatenate | solution.py:228
  652.6 12.9 broadcast_in_dim.126
  665.5 63.3 %scatter_fusion = f32[144,64,768]{2,1,0:T(8,128)} fusion(f32[144,64,768]{2,1,0:T(8,128)} %broadcast_in_dim.126, s32[128]{0:T(128)S(1)} %copy-done.63, f32[128,64,768]{2,1,0:T(8,128)} %pad_maximum_fusion), kind=kCustom, calls=%fused_computation.1 | custom fusion | flops 6291456 | bytes 75497984 | tf_op jit(solution)/shard_map/scatter-add | solution.py:237
  732.7 184.5 %while.43 = (s32[]{:T(128)}, f32[1024,768]{1,0:T(8,128)}, f32[1024,768]{1,0:T(8,128)}, f32[9,1024,768]{2,1,0:T(8,128)}, s32[]{:T(128)}, /*index=5*/s32[]{:T(128)}, s32[]{:T(128)}, s32[]{:T(128)}) while((s32[]{:T(128)}, f32[1024,768]{1,0:T(8,128)}, f32[1024,768]{1,0:T(8,128)}, f32[9,1024,768]{2,1,0:T(8,128)}, s32[]{:T(128)}, ...), condition=%wide.region_20.21_spmd.clone, body=%wide.region_19.20_spmd.clone.sunk | while | flops 6291463 | bytes 37748964 | solution.py:255
  738.9 32.9 %collective-permute-start.3 = (bf16[1024,768]{1,0:T(8,128)(2,1)S(1)}, bf16[1024,768]{1,0:T(8,128)(2,1)}, u32[]{:S(2)}, u32[]{:S(2)}) collective-permute-start(bf16[1024,768]{1,0:T(8,128)(2,1)S(1)} %get-tuple-element.426), channel_id=1, source_target_pairs={{0,2},{2,4},{4,6},{6,8},{8,10},{10,12},{12,14},{14,16},{16,18},{18... | collective-permute-start | bytes 4718600 | tf_op jit(solution)/shard_map/while/body/eval_jaxpr/ppermute | solution.py:15
  778.6 6.7 fusion.116
  786.6 35.1 %collective-permute-start.3 = (bf16[1024,768]{1,0:T(8,128)(2,1)S(1)}, bf16[1024,768]{1,0:T(8,128)(2,1)}, u32[]{:S(2)}, u32[]{:S(2)}) collective-permute-start(bf16[1024,768]{1,0:T(8,128)(2,1)S(1)} %get-tuple-element.426), channel_id=1, source_target_pairs={{0,2},{2,4},{4,6},{6,8},{8,10},{10,12},{12,14},{14,16},{16,18},{18... | collective-permute-start | bytes 4718600 | tf_op jit(solution)/shard_map/while/body/eval_jaxpr/ppermute | solution.py:15
  828.3 6.7 fusion.116
  836.3 35.9 %collective-permute-start.3 = (bf16[1024,768]{1,0:T(8,128)(2,1)S(1)}, bf16[1024,768]{1,0:T(8,128)(2,1)}, u32[]{:S(2)}, u32[]{:S(2)}) collective-permute-start(bf16[1024,768]{1,0:T(8,128)(2,1)S(1)} %get-tuple-element.426), channel_id=1, source_target_pairs={{0,2},{2,4},{4,6},{6,8},{8,10},{10,12},{12,14},{14,16},{16,18},{18... | collective-permute-start | bytes 4718600 | tf_op jit(solution)/shard_map/while/body/eval_jaxpr/ppermute | solution.py:15
  879.0 6.7 fusion.116
  886.9 23.6 %collective-permute-start.3 = (bf16[1024,768]{1,0:T(8,128)(2,1)S(1)}, bf16[1024,768]{1,0:T(8,128)(2,1)}, u32[]{:S(2)}, u32[]{:S(2)}) collective-permute-start(bf16[1024,768]{1,0:T(8,128)(2,1)S(1)} %get-tuple-element.426), channel_id=1, source_target_pairs={{0,2},{2,4},{4,6},{6,8},{8,10},{10,12},{12,14},{14,16},{16,18},{18... | collective-permute-start | bytes 4718600 | tf_op jit(solution)/shard_map/while/body/eval_jaxpr/ppermute | solution.py:15
  922.5 10.8 all_to_all.143
  938.5 11.5 all_to_all.144
  955.4 10.6 fusion.51
  967.5 7.2 fusion.70
  976.6 114.4 %all-reduce.5 = (bf16[768]{0:T(1024)(128)(2,1)S(1)}, bf16[768]{0:T(1024)(128)(2,1)S(1)}, bf16[768]{0:T(1024)(128)(2,1)S(1)}, bf16[768]{0:T(1024)(128)(2,1)S(1)}) all-reduce(f32[768]{0:T(1024)S(1)} %copy-done.49, f32[768]{0:T(1024)S(1)} %copy-done.50, f32[768]{0:T(1024)S(1)} %copy-done.29, ...), channel_id=6, replica_groups=mesh['seq'=16,'head'=2] {'seq'}, use_global_device_ids=true, to_apply=%region_30.31.clone | all-reduce | flops 3072 | bytes 18432
  1091.3 4.9 all-reduce.6
  1103.3 21.2 %reduce-scatter.23.cloned.1.call-done = f32[48,768]{1,0:T(8,128)} async-done(((f32[768,768]{1,0:T(8,128)}), f32[48,768]{1,0:T(8,128)}) %reduce-scatter.23.cloned.1.call-update) | async-done | bytes 147472
  1126.2 112.7 %reduce-scatter.17.cloned.1.call-done = f32[192,768]{1,0:T(8,128)} async-done(((f32[3072,768]{1,0:T(8,128)}), f32[192,768]{1,0:T(8,128)}) %reduce-scatter.17.cloned.1.call-update) | async-done | bytes 589840 | tf_op jit(solution)/shard_map/reduce_scatter | solution.py:292
  1240.7 113.9 %reduce-scatter.15.cloned.1.call-done = f32[48,3072]{1,0:T(8,128)} async-done(((f32[768,3072]{1,0:T(8,128)}), f32[48,3072]{1,0:T(8,128)}) %reduce-scatter.15.cloned.1.call-update) | async-done | bytes 589840 | tf_op jit(solution)/shard_map/reduce_scatter | solution.py:291
  1361.6 42.0 %all-reduce.10.cloned.1.call-done = (bf16[48,768]{0,1:T(8,128)(2,1)}, bf16[48,768]{0,1:T(8,128)(2,1)}, bf16[48,768]{0,1:T(8,128)(2,1)}, bf16[48,768]{1,0:T(8,128...) async-done(((bf16[48,768]{0,1:T(8,128)(2,1)}, bf16[48,768]{0,1:T(8,128)(2,1)}, bf16[48,768]{0,1:T(8,128)(2,1)}, bf16[48,768]{1,0:T(8,128)(2,1)}, ...) | async-done | bytes 884752 | tf_op jit(solution)/shard_map/psum | solution.py:297
  (332 shorter events, 226.6 us)
Async XLA Ops:
  7.2 361.3 %copy-start = (bf16[768,768]{1,0:T(8,128)(2,1)S(1)}, bf16[768,768]{1,0:T(8,128)(2,1)}, u32[]{:S(2)}) copy-start(bf16[768,768]{1,0:T(8,128)(2,1)} %param.23) | copy-start | bytes 3538948
  10.6 15.9 %all-to-all-start = ((bf16[512,2,384]{2,0,1:T(8,128)(2,1)}), bf16[512,2,384]{2,0,1:T(8,128)(2,1)S(1)}, u32[]{:S(2)}, u32[]{:S(2)}) async-start(bf16[512,2,384]{2,0,1:T(8,128)(2,1)} %bitcast.263), calls=%async_computation | async-start | bytes 1572864 | tf_op jit(solution)/shard_map/all_to_all | solution.py:148
  26.5 14.0 all-to-all-start.1
  40.6 244.5 %all-to-all-start.2 = ((bf16[512,2,384]{0,2,1:T(8,128)(2,1)}), bf16[512,2,384]{0,2,1:T(8,128)(2,1)}, u32[]{:S(2)}, u32[]{:S(2)}) async-start(bf16[512,2,384]{0,2,1:T(8,128)(2,1)} %bitcast.40), calls=%async_computation.2 | async-start | bytes 1572864 | tf_op jit(solution)/shard_map/all_to_all | solution.py:147
  54.8 4.5 collective-permute-start
  56.1 7.2 collective-permute-start.1
  70.0 35.6 %collective-permute-start = (bf16[1024,768]{1,0:T(8,128)(2,1)}, bf16[1024,768]{1,0:T(8,128)(2,1)S(1)}, u32[]{:S(2)}, u32[]{:S(2)}) collective-permute-start(bf16[1024,768]{1,0:T(8,128)(2,1)} %get-tuple-element.438), channel_id=1, source_target_pairs={{0,2},{2,4},{4,6},{6,8},{8,10},{10,12},{12,14},{14,16},{16,18},{18... | collective-permute-start | bytes 4718600 | tf_op jit(solution)/shard_map/while/body/eval_jaxpr/ppermute | solution.py:15
  102.5 7.4 collective-permute-start.1
  116.6 22.0 %collective-permute-start = (bf16[1024,768]{1,0:T(8,128)(2,1)}, bf16[1024,768]{1,0:T(8,128)(2,1)S(1)}, u32[]{:S(2)}, u32[]{:S(2)}) collective-permute-start(bf16[1024,768]{1,0:T(8,128)(2,1)} %get-tuple-element.438), channel_id=1, source_target_pairs={{0,2},{2,4},{4,6},{6,8},{8,10},{10,12},{12,14},{14,16},{16,18},{18... | collective-permute-start | bytes 4718600 | tf_op jit(solution)/shard_map/while/body/eval_jaxpr/ppermute | solution.py:15
  135.5 5.6 collective-permute-start.1
  147.8 36.2 %collective-permute-start = (bf16[1024,768]{1,0:T(8,128)(2,1)}, bf16[1024,768]{1,0:T(8,128)(2,1)S(1)}, u32[]{:S(2)}, u32[]{:S(2)}) collective-permute-start(bf16[1024,768]{1,0:T(8,128)(2,1)} %get-tuple-element.438), channel_id=1, source_target_pairs={{0,2},{2,4},{4,6},{6,8},{8,10},{10,12},{12,14},{14,16},{16,18},{18... | collective-permute-start | bytes 4718600 | tf_op jit(solution)/shard_map/while/body/eval_jaxpr/ppermute | solution.py:15
  180.9 5.6 collective-permute-start.1
  288.0 22.2 %copy-start.2 = (bf16[16,64,6,64]{1,0,3,2:T(8,128)(2,1)}, bf16[16,64,6,64]{1,0,3,2:T(8,128)(2,1)S(1)}, u32[]{:S(2)}) copy-start(bf16[16,64,6,64]{1,0,3,2:T(8,128)(2,1)S(1)} %reshape.690) | copy-start | bytes 2359300
  323.5 11.9 copy-start.21
  335.4 16.8 %copy-start.23 = (f32[16,6,64]{2,1,0:T(8,128)}, f32[16,6,64]{2,1,0:T(8,128)S(1)}, u32[]{:S(2)}) copy-start(f32[16,6,64]{2,1,0:T(8,128)S(1)} %fusion.2) | copy-start | bytes 73732
  353.3 15.2 %copy-start.7 = (bf16[512,768]{1,0:T(8,128)(2,1)S(1)}, bf16[512,768]{1,0:T(8,128)(2,1)}, u32[]{:S(2)}) copy-start(bf16[512,768]{1,0:T(8,128)(2,1)} %param.19) | copy-start | bytes 2359300
  356.9 11.5 all-to-all-start.3
  369.4 24.4 %copy-start.11 = (f32[512,768]{1,0:T(8,128)}, f32[512,768]{1,0:T(8,128)S(1)}, u32[]{:S(2)}) copy-start(f32[512,768]{1,0:T(8,128)S(1)} %get-tuple-element.363) | copy-start | bytes 4718596
  369.4 24.4 %copy-start.25 = (f32[512]{0:T(512)}, f32[512]{0:T(512)S(1)}, u32[]{:S(2)}) copy-start(f32[512]{0:T(512)S(1)} %broadcast_multiply_fusion.5) | copy-start | bytes 6148
  369.7 24.1 %copy-start.35 = (f32[512]{0:T(512)}, f32[512]{0:T(512)S(1)}, u32[]{:S(2)}) copy-start(f32[512]{0:T(512)S(1)} %add_rsqrt_fusion.1) | copy-start | bytes 6148
  375.2 14.7 %slice-start.2 = ((s8[4718592]{0:T(1024)(128)(4,1)}), s8[4194304]{0:T(1024)(128)(4,1)S(1)}, s32[]{:S(2)}) async-start(s8[4718592]{0:T(1024)(128)(4,1)} %bitcast.309), calls=%async_computation.23 | async-start | bytes 8388608
  379.1 10.7 copy-start.10
  379.2 10.7 copy-start.27
  394.3 19.2 %copy-start.4 = (f32[512,768]{1,0:T(8,128)}, f32[512,768]{1,0:T(8,128)S(1)}, u32[]{:S(2)}) copy-start(f32[512,768]{1,0:T(8,128)S(1)} %subtract_multiply_fusion) | copy-start | bytes 4718596
  398.3 17.4 %all-to-all-start.4 = ((bf16[512,2,384]{0,2,1:T(8,128)(2,1)}), bf16[512,2,384]{0,2,1:T(8,128)(2,1)S(1)}, u32[]{:S(2)}, u32[]{:S(2)}) async-start(bf16[512,2,384]{0,2,1:T(8,128)(2,1)} %bitcast.285), calls=%async_computation.4 | async-start | bytes 1572864 | tf_op jit(solution)/shard_map/all_to_all | solution.py:204
  401.9 696.4 %reduce-scatter.13.cloned.1.call-start = ((), (), s32[]{:S(2)}) async-start(), calls=%async_computation.14 | async-start | bytes 2506752 | tf_op jit(solution)/shard_map/reduce_scatter | solution.py:288
  480.3 149.9 %all-to-all-start.5 = ((bf16[2,512,384]{1,2,0:T(8,128)(2,1)}), bf16[2,512,384]{1,2,0:T(8,128)(2,1)S(1)}, u32[]{:S(2)}, u32[]{:S(2)}) async-start(bf16[2,512,384]{1,2,0:T(8,128)(2,1)} %copy.185), calls=%async_computation.5 | async-start | bytes 1572864 | tf_op jit(solution)/shard_map/all_to_all | solution.py:262
  483.9 615.9 %reduce-scatter.19.cloned.1.call-start = ((), (), s32[]{:S(2)}) async-start(), calls=%async_computation.17 | async-start | bytes 2506752
  483.9 25.2 %copy-start.3 = (bf16[16,64,6,64]{1,0,3,2:T(8,128)(2,1)S(1)}, bf16[16,64,6,64]{1,0,3,2:T(8,128)(2,1)}, u32[]{:S(2)}) copy-start(bf16[16,64,6,64]{1,0,3,2:T(8,128)(2,1)} %copy-done.2) | copy-start | bytes 2359300
  605.1 26.1 %copy-start.8 = (bf16[512,768]{1,0:T(8,128)(2,1)S(1)}, bf16[512,768]{1,0:T(8,128)(2,1)}, u32[]{:S(2)}) copy-start(bf16[512,768]{1,0:T(8,128)(2,1)} %param.19) | copy-start | bytes 2359300
  635.1 466.5 %reduce-scatter.21.cloned.1.call-start = ((), (), s32[]{:S(2)}) async-start(), calls=%async_computation.18 | async-start | bytes 2506752
  652.6 12.9 copy-start.63
  737.7 34.3 %collective-permute-start.2 = (bf16[1024,768]{1,0:T(8,128)(2,1)}, bf16[1024,768]{1,0:T(8,128)(2,1)}, u32[]{:S(2)}, u32[]{:S(2)}) collective-permute-start(bf16[1024,768]{1,0:T(8,128)(2,1)} %get-tuple-element.425), channel_id=1, source_target_pairs={{2,0},{4,2},{6,4},{8,6},{10,8},{12,10},{14,12},{16,14},{18,16},{20... | collective-permute-start | bytes 4718600 | tf_op jit(solution)/shard_map/while/body/eval_jaxpr/ppermute | solution.py:15
  738.9 36.3 %collective-permute-start.3 = (bf16[1024,768]{1,0:T(8,128)(2,1)S(1)}, bf16[1024,768]{1,0:T(8,128)(2,1)}, u32[]{:S(2)}, u32[]{:S(2)}) collective-permute-start(bf16[1024,768]{1,0:T(8,128)(2,1)S(1)} %get-tuple-element.426), channel_id=1, source_target_pairs={{0,2},{2,4},{4,6},{6,8},{8,10},{10,12},{12,14},{14,16},{16,18},{18... | collective-permute-start | bytes 4718600 | tf_op jit(solution)/shard_map/while/body/eval_jaxpr/ppermute | solution.py:15
  785.3 36.5 %collective-permute-start.2 = (bf16[1024,768]{1,0:T(8,128)(2,1)}, bf16[1024,768]{1,0:T(8,128)(2,1)}, u32[]{:S(2)}, u32[]{:S(2)}) collective-permute-start(bf16[1024,768]{1,0:T(8,128)(2,1)} %get-tuple-element.425), channel_id=1, source_target_pairs={{2,0},{4,2},{6,4},{8,6},{10,8},{12,10},{14,12},{16,14},{18,16},{20... | collective-permute-start | bytes 4718600 | tf_op jit(solution)/shard_map/while/body/eval_jaxpr/ppermute | solution.py:15
  786.6 38.5 %collective-permute-start.3 = (bf16[1024,768]{1,0:T(8,128)(2,1)S(1)}, bf16[1024,768]{1,0:T(8,128)(2,1)}, u32[]{:S(2)}, u32[]{:S(2)}) collective-permute-start(bf16[1024,768]{1,0:T(8,128)(2,1)S(1)} %get-tuple-element.426), channel_id=1, source_target_pairs={{0,2},{2,4},{4,6},{6,8},{8,10},{10,12},{12,14},{14,16},{16,18},{18... | collective-permute-start | bytes 4718600 | tf_op jit(solution)/shard_map/while/body/eval_jaxpr/ppermute | solution.py:15
  835.0 37.3 %collective-permute-start.2 = (bf16[1024,768]{1,0:T(8,128)(2,1)}, bf16[1024,768]{1,0:T(8,128)(2,1)}, u32[]{:S(2)}, u32[]{:S(2)}) collective-permute-start(bf16[1024,768]{1,0:T(8,128)(2,1)} %get-tuple-element.425), channel_id=1, source_target_pairs={{2,0},{4,2},{6,4},{8,6},{10,8},{12,10},{14,12},{16,14},{18,16},{20... | collective-permute-start | bytes 4718600 | tf_op jit(solution)/shard_map/while/body/eval_jaxpr/ppermute | solution.py:15
  836.3 39.3 %collective-permute-start.3 = (bf16[1024,768]{1,0:T(8,128)(2,1)S(1)}, bf16[1024,768]{1,0:T(8,128)(2,1)}, u32[]{:S(2)}, u32[]{:S(2)}) collective-permute-start(bf16[1024,768]{1,0:T(8,128)(2,1)S(1)} %get-tuple-element.426), channel_id=1, source_target_pairs={{0,2},{2,4},{4,6},{6,8},{8,10},{10,12},{12,14},{14,16},{16,18},{18... | collective-permute-start | bytes 4718600 | tf_op jit(solution)/shard_map/while/body/eval_jaxpr/ppermute | solution.py:15
  885.6 25.0 %collective-permute-start.2 = (bf16[1024,768]{1,0:T(8,128)(2,1)}, bf16[1024,768]{1,0:T(8,128)(2,1)}, u32[]{:S(2)}, u32[]{:S(2)}) collective-permute-start(bf16[1024,768]{1,0:T(8,128)(2,1)} %get-tuple-element.425), channel_id=1, source_target_pairs={{2,0},{4,2},{6,4},{8,6},{10,8},{12,10},{14,12},{16,14},{18,16},{20... | collective-permute-start | bytes 4718600 | tf_op jit(solution)/shard_map/while/body/eval_jaxpr/ppermute | solution.py:15
  886.9 27.0 %collective-permute-start.3 = (bf16[1024,768]{1,0:T(8,128)(2,1)S(1)}, bf16[1024,768]{1,0:T(8,128)(2,1)}, u32[]{:S(2)}, u32[]{:S(2)}) collective-permute-start(bf16[1024,768]{1,0:T(8,128)(2,1)S(1)} %get-tuple-element.426), channel_id=1, source_target_pairs={{0,2},{2,4},{4,6},{6,8},{8,10},{10,12},{12,14},{14,16},{16,18},{18... | collective-permute-start | bytes 4718600 | tf_op jit(solution)/shard_map/while/body/eval_jaxpr/ppermute | solution.py:15
  938.4 186.1 %reduce-scatter.23.cloned.1.call-start = ((), (), s32[]{:S(2)}) async-start(), calls=%async_computation.19 | async-start | bytes 2506752
  955.1 283.8 %reduce-scatter.17.cloned.1.call-start = ((), (), s32[]{:S(2)}) async-start(), calls=%async_computation.16 | async-start | bytes 10027008 | tf_op jit(solution)/shard_map/reduce_scatter | solution.py:292
  966.1 388.4 %reduce-scatter.15.cloned.1.call-start = ((), (), s32[]{:S(2)}) async-start(), calls=%async_computation.15 | async-start | bytes 10027008 | tf_op jit(solution)/shard_map/reduce_scatter | solution.py:291
  974.7 381.7 %copy-start.16 = (bf16[2,512,384]{1,2,0:T(8,128)(2,1)S(1)}, bf16[2,512,384]{1,2,0:T(8,128)(2,1)}, u32[]{:S(2)}) copy-start(bf16[2,512,384]{1,2,0:T(8,128)(2,1)} %copy-done.15) | copy-start | bytes 2359300
  974.7 381.7 %copy-start.64 = (bf16[768,768]{1,0:T(8,128)(2,1)S(1)}, bf16[768,768]{1,0:T(8,128)(2,1)}, u32[]{:S(2)}) copy-start(bf16[768,768]{1,0:T(8,128)(2,1)} %param.20) | copy-start | bytes 3538948
  974.7 428.9 %all-reduce.10.cloned.1.call-start = ((), (), s32[]{:S(2)}) async-start(), calls=%async_computation.20 | async-start | bytes 2506752 | tf_op jit(solution)/shard_map/psum | solution.py:297
  1240.7 116.6 %copy-start.17 = (bf16[512,2,384]{0,2,1:T(8,128)(2,1)S(1)}, bf16[512,2,384]{0,2,1:T(8,128)(2,1)}, u32[]{:S(2)}) copy-start(bf16[512,2,384]{0,2,1:T(8,128)(2,1)} %copy.194) | copy-start | bytes 2359300
  1359.6 54.3 %copy-start.1 = (bf16[768,768]{1,0:T(8,128)(2,1)S(1)}, bf16[768,768]{1,0:T(8,128)(2,1)}, u32[]{:S(2)}) copy-start(bf16[768,768]{1,0:T(8,128)(2,1)} %param.23) | copy-start | bytes 3538948
  (57 other events, 232.7 us)
Sparse Core Ops, SparseCore 0:
  415.9 115.2 reduce-scatter.12
  635.2 115.9 reduce-scatter.18
  938.5 119.8 reduce-scatter.20
  1062.6 61.9 reduce-scatter.22
  1128.5 110.3 reduce-scatter.16
  1243.4 111.1 reduce-scatter.14
  1358.3 45.1 all-reduce.9
where the time goes:
time: 1430 us; the launch traced here: 1420 us
  local copies, waits for them, and re-layouts  338 us (24%)
  waiting for transfers between devices  322 us (23%)
  starting transfers between devices  247 us (17%)
  other arithmetic  192 us (13%)
  matrix products  164 us (11%)
  blocking collectives  142 us (10%)
  between operations  16.2 us (1%)
    ppermute x16, starting transfers between devices, shifted(): lax.ppermute(value, axis, [(source, source + steps) for source in range(f...  224 us
    unnamed x1, blocking collectives  114 us
    reduce_scatter x1, waiting for transfers between devices, body(): lax.psum_scatter(grad_terms[6], 'seq', scatter_dimension=0, tiled=True)  114 us
    reduce_scatter x1, waiting for transfers between devices, body(): lax.psum_scatter(grad_terms[7], 'seq', scatter_dimension=0, tiled=True)  113 us
    scatter-add x1, other arithmetic, body(): grad_buffer.at[local_rows.reshape(-1)]  63.3 us
    unnamed x169, local copies, waits for them, and re-layouts  56 us
    concatenate x2, local copies, waits for them, and re-layouts, body(): jnp.concatenate([grad_key_rows.reshape(stretch_blocks, slot_count, BLK, -...  50.3 us
    psum x1, waiting for transfers between devices, body(): lax.psum(shares[0].astype(jnp.bfloat16), 'head').astype(jnp.float32)  42 us
  transfers between devices with their start and end apart: 29, of which 19 were waited for; matrix products, arithmetic and copies ran while one was open for 40% of the time, Pallas kernels for 0%

commit v1 on v0

--- a/solution.py
+++ b/solution.py
@@ -7,6 +7,7 @@
 BLK = 64
 MAXB = 64
 eps_norm = 1e-06
+manage_tracks = lambda inner_x: lax.all_gather(inner_x, "head").sum(axis=0)
 
 
 def shifted(value, axis, steps):
@@ -294,7 +295,7 @@
         lax.psum_scatter(grad_terms[9], "seq", scatter_dimension=0, tiled=True),
     )
     totals = (
-        lax.psum(shares[0].astype(jnp.bfloat16), "head").astype(jnp.float32),
+        manage_tracks(shares[0].astype(jnp.bfloat16)).astype(jnp.float32),
         lax.psum(shares[1].astype(jnp.bfloat16), "head").astype(jnp.float32),
         lax.psum(shares[2].astype(jnp.bfloat16), "head").astype(jnp.float32),
         lax.psum(shares[3].astype(jnp.bfloat16), "head").astype(jnp.float32),

time: 1430 us -> 1480 us (1.035)
  waiting for transfers between devices: 322 us -> 352 us
  starting transfers between devices: 247 us -> 267 us
    reduce_scatter x0 -> x1, waiting for transfers between devices: none -> 59.8 us  [body(): lax.psum_scatter(grad_terms[0], 'seq', scatter_dimension=0, tiled=True)]
    ppermute x16, starting transfers between devices: 224 us -> 248 us  [shifted(): lax.ppermute(value, axis, [(source, source + steps) for source in range(f...]
    unnamed x10 -> x9, waiting for transfers between devices: 21.3 us -> 2.77 us
    unnamed x169 -> x165, local copies, waits for them, and re-layouts: 56 us -> 52.9 us
  transfers between devices with their start and end apart: 29 -> 28, of which waited for: 19 -> 16; matrix products, arithmetic and copies ran while one was open for 40% -> 30% of each run, Pallas kernels for 0% -> 0%
where the time goes in v1:
time: 1480 us; the launch traced here: 1470 us
  waiting for transfers between devices  352 us (24%)
  local copies, waits for them, and re-layouts  336 us (23%)
  starting transfers between devices  267 us (18%)
  other arithmetic  193 us (13%)
  matrix products  162 us (11%)
  blocking collectives  147 us (10%)
  between operations  16.1 us (1%)
    ppermute x16, starting transfers between devices, shifted(): lax.ppermute(value, axis, [(source, source + steps) for source in range(f...  248 us
    reduce_scatter x1, waiting for transfers between devices, body(): lax.psum_scatter(grad_terms[6], 'seq', scatter_dimension=0, tiled=True)  113 us
    reduce_scatter x1, waiting for transfers between devices, body(): lax.psum_scatter(grad_terms[7], 'seq', scatter_dimension=0, tiled=True)  113 us
    unnamed x1, blocking collectives  100 us
    scatter-add x1, other arithmetic, body(): grad_buffer.at[local_rows.reshape(-1)]  63.2 us
    reduce_scatter x1, waiting for transfers between devices, body(): lax.psum_scatter(grad_terms[0], 'seq', scatter_dimension=0, tiled=True)  59.8 us
    unnamed x165, local copies, waits for them, and re-layouts  52.9 us
    concatenate x2, local copies, waits for them, and re-layouts, body(): jnp.concatenate([grad_key_rows.reshape(stretch_blocks, slot_count, BLK, -...  50.4 us
  transfers between devices with their start and end apart: 28, of which 16 were waited for; matrix products, arithmetic and copies ran while one was open for 30% of the time, Pallas kernels for 0%

profile of v1, /device:TPU:0, one launch (start us, length us, event | category | flops | bytes accessed | tf_op | source)
XLA Modules:
  0.0 1473.0 jit_solution(799116442904613278)
XLA Ops:
  20.6 6.0 all-to-all-done.2
  33.1 7.7 all-to-all-done
  61.1 6.0 dynamic_update_slice.22
  67.1 151.4 %while.42 = (s32[]{:T(128)}, bf16[1024,768]{1,0:T(8,128)(2,1)}, bf16[1024,768]{1,0:T(8,128)(2,1)}, bf16[9,1024,768]{2,1,0:T(8,128)(2,1)}, s32[]{:T(128)}, /*inde...) while((s32[]{:T(128)}, bf16[1024,768]{1,0:T(8,128)(2,1)}, bf16[1024,768]{1,0:T(8,128)(2,1)}, ...), condition=%wide.region_1.2_spmd, body=%wide.region_0.1_spmd.sunk | while | flops 10 | bytes 25166108 | solution.py:106
  82.7 50.9 %collective-permute-start = (bf16[1024,768]{1,0:T(8,128)(2,1)}, bf16[1024,768]{1,0:T(8,128)(2,1)}, u32[]{:S(2)}, u32[]{:S(2)}) collective-permute-start(bf16[1024,768]{1,0:T(8,128)(2,1)} %get-tuple-element.449), channel_id=1, source_target_pairs={{0,2},{2,4},{4,6},{6,8},{8,10},{10,12},{12,14},{14,16},{16,18},{18... | collective-permute-start | bytes 4718600 | tf_op jit(solution)/shard_map/while/body/eval_jaxpr/ppermute | solution.py:16
  143.6 20.5 %collective-permute-start = (bf16[1024,768]{1,0:T(8,128)(2,1)}, bf16[1024,768]{1,0:T(8,128)(2,1)}, u32[]{:S(2)}, u32[]{:S(2)}) collective-permute-start(bf16[1024,768]{1,0:T(8,128)(2,1)} %get-tuple-element.449), channel_id=1, source_target_pairs={{0,2},{2,4},{4,6},{6,8},{8,10},{10,12},{12,14},{14,16},{16,18},{18... | collective-permute-start | bytes 4718600 | tf_op jit(solution)/shard_map/while/body/eval_jaxpr/ppermute | solution.py:16
  174.3 35.4 %collective-permute-start = (bf16[1024,768]{1,0:T(8,128)(2,1)}, bf16[1024,768]{1,0:T(8,128)(2,1)}, u32[]{:S(2)}, u32[]{:S(2)}) collective-permute-start(bf16[1024,768]{1,0:T(8,128)(2,1)} %get-tuple-element.449), channel_id=1, source_target_pairs={{0,2},{2,4},{4,6},{6,8},{8,10},{10,12},{12,14},{14,16},{16,18},{18... | collective-permute-start | bytes 4718600 | tf_op jit(solution)/shard_map/while/body/eval_jaxpr/ppermute | solution.py:16
  218.4 13.2 gather_fusion
  231.7 39.0 %reshape.689 = bf16[16,8,64,2,6,64]{5,4,3,2,1,0:T(8,128)(2,1)} reshape(bf16[128,64,768]{2,1,0:T(8,128)(2,1)} %gather_fusion) | data formatting | bytes 25165824 | tf_op jit(solution)/shard_map/reshape | solution.py:113
  270.7 28.5 %slice_bitcast_fusion = (bf16[16,8,64,6,64]{4,3,2,1,0:T(8,128)(2,1)}, bf16[16,8,64,1,6,64]{5,4,3,2,1,0:T(8,128)(2,1)}, bf16[16,8,64,1,6,64]{5,4,3,2,1,0:T(8,128)(2,1)}) fusion(bf16[16,8,64,2,6,64]{5,4,3,2,1,0:T(8,128)(2,1)} %reshape.689), kind=kLoop, calls=%fused_computation.149 | loop fusion | bytes 31457280 | tf_op jit(solution)/shard_map/squeeze | solution.py:114
  299.1 11.3 copy.267
  310.4 21.7 %copy.266 = bf16[16,8,64,1,6,64]{2,5,1,4,0,3:T(8,128)(2,1)} copy(bf16[16,8,64,1,6,64]{5,4,3,2,1,0:T(8,128)(2,1)} %get-tuple-element.354) | data formatting | bytes 12582912
  332.1 13.3 fusion.11
  345.4 11.9 fusion.2
  357.3 16.6 %fusion.44 = bf16[16,64,6,64]{1,3,2,0:T(8,128)(2,1)S(1)} fusion(f32[16,6,64]{2,1,0:T(8,128)S(1)} %fusion.2, f32[16,6,64]{2,1,0:T(8,128)S(1)} %get-tuple-element.371, f32[16,6,64,8,64]{2,4,3,1,0:T(8,128)} %bitcast.271, pred[16,8]{1,0:T(8,128)(4,1)S(1)} %copy.215, bf16[16,8,64,1,6,64]{2,5,1,4,0,3:T(8,128)(2,1)} %copy.266), kind=kOutput, calls=%fused_computation.71 | convolution fusion | flops 418775040 | bytes 19710080 | tf_op jit(solution)/shard_map/chqsk,cskhd->cqhd/dot_general | solution.py:173
  383.0 7.2 all-to-all-done.3
  403.5 8.1 fusion.21
  423.7 11.6 copy.226
  439.4 24.1 %multiply_reduce_fusion = (f32[16,6,64]{2,1,0:T(8,128)S(1)}, f32[16,6,64,512]{2,3,1,0}) fusion(f32[16,6,64]{2,1,0:T(8,128)S(1)} %log_add_fusion, pred[16,8]{1,0:T(8,128)(4,1)S(1)} %copy.215, f32[16,6,64,512]{2,3,1,0} %get-tuple-element.372, bf16[16,6,64,512]{2,3,1,0:T(8,128)(2,1)} %bitcast.276, bf16[16,64,6,64]{1,0,3,2:T(8,128)(2,1)S(1)} %reshape.691), kind=kOutput, calls=%fused_computation.11 | convolution fusion | flops 418375680 | bytes 32292992
  463.6 24.4 %fusion.12 = f32[16,8,64,6,64]{2,4,1,3,0:T(8,128)} fusion(f32[16,6,64]{2,1,0:T(8,128)S(1)} %log_add_fusion, f32[16,6,64,8,64]{2,4,3,1,0:T(8,128)} %bitcast.272, pred[16,8]{1,0:T(8,128)(4,1)S(1)} %copy.215, bf16[16,64,6,64,1]{1,0,3,2,4:T(8,128)(2,1)S(1)} %bitcast.278), kind=kOutput, calls=%fused_computation.27 | convolution fusion | flops 415236096 | bytes 25976960 | tf_op jit(solution)/shard_map/chqsk,cqhd->cskhd/dot_general | solution.py:216
  488.0 29.1 %copy.238 = f32[16,8,64,6,64]{4,3,2,1,0:T(8,128)} copy(f32[16,8,64,6,64]{2,4,1,3,0:T(8,128)} %fusion.12) | data formatting | bytes 25165824 | tf_op jit(solution)/shard_map/chqsk,cqhd->cskhd/transpose | solution.py:216
  517.0 25.2 %concatenate.52 = f32[128,64,384]{2,1,0:T(8,128)} reshape(f32[16,8,64,6,64]{4,3,2,1,0:T(8,128)} %copy.238) | data formatting | bytes 25165824 | tf_op jit(solution)/shard_map/concatenate | solution.py:229
  542.3 22.0 %multiply_convert_fusion = bf16[16,6,64,8,64]{2,4,3,1,0:T(8,128)(2,1)} fusion(f32[16,6,64]{2,1,0:T(8,128)S(1)} %get-tuple-element.378, f32[16,6,64]{2,1,0:T(8,128)S(1)} %log_add_fusion, pred[16,8]{1,0:T(8,128)(4,1)S(1)} %copy.215, f32[16,6,64,512]{2,3,1,0} %get-tuple-element.379, f32[16,6,64,512]{2,3,1,0} %get-tuple-element.372), kind=kLoop, calls=%fused_computation.10 | loop fusion | flops 18874368 | bytes 31506560 | tf_op jit(solution)/shard_map/convert_element_type | solution.py:220
  564.2 12.9 multiply_bitcast_fusion
  577.1 29.5 %copy.235 = f32[16,8,64,6,64]{4,3,2,1,0:T(8,128)} copy(f32[16,8,64,6,64]{4,2,1,3,0:T(8,128)} %multiply_bitcast_fusion) | data formatting | bytes 25165824 | tf_op jit(solution)/shard_map/mul | solution.py:226
  606.6 25.1 %concatenate.51 = f32[128,64,384]{2,1,0:T(8,128)} reshape(f32[16,8,64,6,64]{4,3,2,1,0:T(8,128)} %copy.235) | data formatting | bytes 25165824 | tf_op jit(solution)/shard_map/concatenate | solution.py:229
  631.8 17.4 %pad_maximum_fusion = f32[128,64,768]{2,1,0:T(8,128)} fusion(f32[128,64,384]{2,1,0:T(8,128)} %concatenate.52, f32[128,64,384]{2,1,0:T(8,128)} %concatenate.51), kind=kLoop, calls=%fused_computation.8 | loop fusion | flops 6291456 | bytes 50331648 | tf_op jit(solution)/shard_map/concatenate | solution.py:229
  649.1 12.9 broadcast_in_dim.126
  662.0 63.2 %scatter_fusion = f32[144,64,768]{2,1,0:T(8,128)} fusion(f32[144,64,768]{2,1,0:T(8,128)} %broadcast_in_dim.126, s32[128]{0:T(128)S(1)} %copy-done.62, f32[128,64,768]{2,1,0:T(8,128)} %pad_maximum_fusion), kind=kCustom, calls=%fused_computation.1 | custom fusion | flops 6291456 | bytes 75497984 | tf_op jit(solution)/shard_map/scatter-add | solution.py:238
  729.0 184.3 %while.43 = (s32[]{:T(128)}, f32[1024,768]{1,0:T(8,128)}, f32[1024,768]{1,0:T(8,128)}, f32[9,1024,768]{2,1,0:T(8,128)}, s32[]{:T(128)}, /*index=5*/s32[]{:T(128)}, s32[]{:T(128)}, s32[]{:T(128)}) while((s32[]{:T(128)}, f32[1024,768]{1,0:T(8,128)}, f32[1024,768]{1,0:T(8,128)}, f32[9,1024,768]{2,1,0:T(8,128)}, s32[]{:T(128)}, ...), condition=%wide.region_20.21_spmd.clone, body=%wide.region_19.20_spmd.clone.sunk | while | flops 6291463 | bytes 37748964 | solution.py:256
  735.2 35.0 %collective-permute-start.3 = (bf16[1024,768]{1,0:T(8,128)(2,1)S(1)}, bf16[1024,768]{1,0:T(8,128)(2,1)}, u32[]{:S(2)}, u32[]{:S(2)}) collective-permute-start(bf16[1024,768]{1,0:T(8,128)(2,1)S(1)} %get-tuple-element.437), channel_id=1, source_target_pairs={{0,2},{2,4},{4,6},{6,8},{8,10},{10,12},{12,14},{14,16},{16,18},{18... | collective-permute-start | bytes 4718600 | tf_op jit(solution)/shard_map/while/body/eval_jaxpr/ppermute | solution.py:16
  776.9 6.7 fusion.116
  784.9 36.3 %collective-permute-start.3 = (bf16[1024,768]{1,0:T(8,128)(2,1)S(1)}, bf16[1024,768]{1,0:T(8,128)(2,1)}, u32[]{:S(2)}, u32[]{:S(2)}) collective-permute-start(bf16[1024,768]{1,0:T(8,128)(2,1)S(1)} %get-tuple-element.437), channel_id=1, source_target_pairs={{0,2},{2,4},{4,6},{6,8},{8,10},{10,12},{12,14},{14,16},{16,18},{18... | collective-permute-start | bytes 4718600 | tf_op jit(solution)/shard_map/while/body/eval_jaxpr/ppermute | solution.py:16
  828.0 6.7 fusion.116
  836.0 21.6 %collective-permute-start.3 = (bf16[1024,768]{1,0:T(8,128)(2,1)S(1)}, bf16[1024,768]{1,0:T(8,128)(2,1)}, u32[]{:S(2)}, u32[]{:S(2)}) collective-permute-start(bf16[1024,768]{1,0:T(8,128)(2,1)S(1)} %get-tuple-element.437), channel_id=1, source_target_pairs={{0,2},{2,4},{4,6},{6,8},{8,10},{10,12},{12,14},{14,16},{16,18},{18... | collective-permute-start | bytes 4718600 | tf_op jit(solution)/shard_map/while/body/eval_jaxpr/ppermute | solution.py:16
  864.4 6.7 fusion.116
  872.4 34.1 %collective-permute-start.3 = (bf16[1024,768]{1,0:T(8,128)(2,1)S(1)}, bf16[1024,768]{1,0:T(8,128)(2,1)}, u32[]{:S(2)}, u32[]{:S(2)}) collective-permute-start(bf16[1024,768]{1,0:T(8,128)(2,1)S(1)} %get-tuple-element.437), channel_id=1, source_target_pairs={{0,2},{2,4},{4,6},{6,8},{8,10},{10,12},{12,14},{14,16},{16,18},{18... | collective-permute-start | bytes 4718600 | tf_op jit(solution)/shard_map/while/body/eval_jaxpr/ppermute | solution.py:16
  918.6 11.2 all_to_all.143
  934.9 15.1 %all_to_all.144 = bf16[2,512,384]{2,1,0:T(8,128)(2,1)S(1)} all-to-all(bf16[2,512,384]{2,1,0:T(8,128)(2,1)} %bitcast.292), channel_id=1, replica_groups=mesh['seq'=16,'head'=2] {'head'}, dimensions={0} | all-to-all | bytes 1572864 | tf_op jit(solution)/shard_map/all_to_all | solution.py:264
  955.3 10.8 fusion.51
  967.6 7.2 fusion.70
  974.9 10.7 fusion.41
  987.5 10.4 all_to_all.145
  1003.0 100.4 %all-reduce.5 = (bf16[768]{0:T(1024)(128)(2,1)S(1)}, bf16[768]{0:T(1024)(128)(2,1)S(1)}, bf16[768]{0:T(1024)(128)(2,1)S(1)}, bf16[768]{0:T(1024)(128)(2,1)S(1)}) all-reduce(f32[768]{0:T(1024)S(1)} %copy-done.49, f32[768]{0:T(1024)S(1)} %copy-done.50, f32[768]{0:T(1024)S(1)} %copy-done.29, ...), channel_id=7, replica_groups=mesh['seq'=16,'head'=2] {'seq'}, use_global_device_ids=true, to_apply=%region_30.31.clone | all-reduce | flops 3072 | bytes 18432
  1118.5 113.2 %reduce-scatter.17.cloned.1.call-done = f32[192,768]{1,0:T(8,128)} async-done(((f32[3072,768]{1,0:T(8,128)}), f32[192,768]{1,0:T(8,128)}) %reduce-scatter.17.cloned.1.call-update) | async-done | bytes 589840 | tf_op jit(solution)/shard_map/reduce_scatter | solution.py:293
  1233.5 113.3 %reduce-scatter.15.cloned.1.call-done = f32[48,3072]{1,0:T(8,128)} async-done(((f32[768,3072]{1,0:T(8,128)}), f32[48,3072]{1,0:T(8,128)}) %reduce-scatter.15.cloned.1.call-update) | async-done | bytes 589840 | tf_op jit(solution)/shard_map/reduce_scatter | solution.py:292
  1353.8 59.8 %reduce-scatter.19.cloned.1.call-done = f32[48,768]{1,0:T(8,128)} async-done(((f32[768,768]{1,0:T(8,128)}), f32[48,768]{1,0:T(8,128)}) %reduce-scatter.19.cloned.1.call-update) | async-done | bytes 147472 | tf_op jit(solution)/shard_map/reduce_scatter | solution.py:286
  1420.3 37.1 %all-reduce.10.cloned.1.call-done = (bf16[48,768]{0,1:T(8,128)(2,1)}, bf16[48,768]{0,1:T(8,128)(2,1)}, bf16[48,768]{1,0:T(8,128)(2,1)}, bf16[48,3072]{1,0:T(8,128)(2,1)}, bf16[192,768]{1,0:T(8,128)(2,1)}) async-done(((bf16[48,768]{0,1:T(8,128)(2,1)}, bf16[48,768]{0,1:T(8,128)(2,1)}, bf16[48,768]{1,0:T(8,128)(2,1)}, bf16[48,3072]{1,0:T(8,128)(2,1)}, bf16[192,768]{1,0:T(8,128)(2,1)}), ...) | async-done | bytes 811024 | tf_op jit(solution)/shard_map/psum | solution.py:299
  (331 shorter events, 225.9 us)
Async XLA Ops:
  7.2 383.0 %copy-start = (bf16[768,768]{1,0:T(8,128)(2,1)S(1)}, bf16[768,768]{1,0:T(8,128)(2,1)}, u32[]{:S(2)}) copy-start(bf16[768,768]{1,0:T(8,128)(2,1)} %param.23) | copy-start | bytes 3538948
  10.8 15.8 %all-to-all-start.2 = ((bf16[512,2,384]{0,2,1:T(8,128)(2,1)}), bf16[512,2,384]{0,2,1:T(8,128)(2,1)S(1)}, u32[]{:S(2)}, u32[]{:S(2)}) async-start(bf16[512,2,384]{0,2,1:T(8,128)(2,1)} %bitcast.40), calls=%async_computation.2 | async-start | bytes 1572864 | tf_op jit(solution)/shard_map/all_to_all | solution.py:148
  15.6 17.4 %copy-start.32 = (s32[16]{0:T(128)}, s32[16]{0:T(128)S(1)}, u32[]{:S(2)}) copy-start(s32[16]{0:T(128)S(1)} %get-tuple-element.311) | copy-start | bytes 196
  26.6 14.2 all-to-all-start
  33.0 13.5 copy-start.39
  40.8 15.8 %all-to-all-start.1 = ((bf16[512,2,384]{2,0,1:T(8,128)(2,1)}), bf16[512,2,384]{2,0,1:T(8,128)(2,1)S(1)}, u32[]{:S(2)}, u32[]{:S(2)}) async-start(bf16[512,2,384]{2,0,1:T(8,128)(2,1)} %bitcast.286), calls=%async_computation.1 | async-start | bytes 1572864 | tf_op jit(solution)/shard_map/all_to_all | solution.py:150
  67.1 5.5 collective-permute-start.1
  68.3 6.4 collective-permute-start
  81.4 52.2 %collective-permute-start.1 = (bf16[1024,768]{1,0:T(8,128)(2,1)}, bf16[1024,768]{1,0:T(8,128)(2,1)S(1)}, u32[]{:S(2)}, u32[]{:S(2)}) collective-permute-start(bf16[1024,768]{1,0:T(8,128)(2,1)} %get-tuple-element.450), channel_id=1, source_target_pairs={{2,0},{4,2},{6,4},{8,6},{10,8},{12,10},{14,12},{16,14},{18,16},{20... | collective-permute-start | bytes 4718600 | tf_op jit(solution)/shard_map/while/body/eval_jaxpr/ppermute | solution.py:16
  82.7 53.1 %collective-permute-start = (bf16[1024,768]{1,0:T(8,128)(2,1)}, bf16[1024,768]{1,0:T(8,128)(2,1)}, u32[]{:S(2)}, u32[]{:S(2)}) collective-permute-start(bf16[1024,768]{1,0:T(8,128)(2,1)} %get-tuple-element.449), channel_id=1, source_target_pairs={{0,2},{2,4},{4,6},{6,8},{8,10},{10,12},{12,14},{14,16},{16,18},{18... | collective-permute-start | bytes 4718600 | tf_op jit(solution)/shard_map/while/body/eval_jaxpr/ppermute | solution.py:16
  142.4 21.8 %collective-permute-start.1 = (bf16[1024,768]{1,0:T(8,128)(2,1)}, bf16[1024,768]{1,0:T(8,128)(2,1)S(1)}, u32[]{:S(2)}, u32[]{:S(2)}) collective-permute-start(bf16[1024,768]{1,0:T(8,128)(2,1)} %get-tuple-element.450), channel_id=1, source_target_pairs={{2,0},{4,2},{6,4},{8,6},{10,8},{12,10},{14,12},{16,14},{18,16},{20... | collective-permute-start | bytes 4718600 | tf_op jit(solution)/shard_map/while/body/eval_jaxpr/ppermute | solution.py:16
  143.6 22.7 %collective-permute-start = (bf16[1024,768]{1,0:T(8,128)(2,1)}, bf16[1024,768]{1,0:T(8,128)(2,1)}, u32[]{:S(2)}, u32[]{:S(2)}) collective-permute-start(bf16[1024,768]{1,0:T(8,128)(2,1)} %get-tuple-element.449), channel_id=1, source_target_pairs={{0,2},{2,4},{4,6},{6,8},{8,10},{10,12},{12,14},{14,16},{16,18},{18... | collective-permute-start | bytes 4718600 | tf_op jit(solution)/shard_map/while/body/eval_jaxpr/ppermute | solution.py:16
  173.0 36.7 %collective-permute-start.1 = (bf16[1024,768]{1,0:T(8,128)(2,1)}, bf16[1024,768]{1,0:T(8,128)(2,1)S(1)}, u32[]{:S(2)}, u32[]{:S(2)}) collective-permute-start(bf16[1024,768]{1,0:T(8,128)(2,1)} %get-tuple-element.450), channel_id=1, source_target_pairs={{2,0},{4,2},{6,4},{8,6},{10,8},{12,10},{14,12},{16,14},{18,16},{20... | collective-permute-start | bytes 4718600 | tf_op jit(solution)/shard_map/while/body/eval_jaxpr/ppermute | solution.py:16
  174.3 37.6 %collective-permute-start = (bf16[1024,768]{1,0:T(8,128)(2,1)}, bf16[1024,768]{1,0:T(8,128)(2,1)}, u32[]{:S(2)}, u32[]{:S(2)}) collective-permute-start(bf16[1024,768]{1,0:T(8,128)(2,1)} %get-tuple-element.449), channel_id=1, source_target_pairs={{0,2},{2,4},{4,6},{6,8},{8,10},{10,12},{12,14},{14,16},{16,18},{18... | collective-permute-start | bytes 4718600 | tf_op jit(solution)/shard_map/while/body/eval_jaxpr/ppermute | solution.py:16
  310.4 21.7 %copy-start.2 = (bf16[16,64,6,64]{1,0,3,2:T(8,128)(2,1)S(1)}, bf16[16,64,6,64]{1,0,3,2:T(8,128)(2,1)}, u32[]{:S(2)}) copy-start(bf16[16,64,6,64]{1,0,3,2:T(8,128)(2,1)} %reshape.690) | copy-start | bytes 2359300
  345.4 11.9 copy-start.21
  357.3 16.7 %copy-start.23 = (f32[16,6,64]{2,1,0:T(8,128)}, f32[16,6,64]{2,1,0:T(8,128)S(1)}, u32[]{:S(2)}) copy-start(f32[16,6,64]{2,1,0:T(8,128)S(1)} %fusion.2) | copy-start | bytes 73732
  375.0 15.2 %copy-start.7 = (bf16[512,768]{1,0:T(8,128)(2,1)S(1)}, bf16[512,768]{1,0:T(8,128)(2,1)}, u32[]{:S(2)}) copy-start(bf16[512,768]{1,0:T(8,128)(2,1)} %param.19) | copy-start | bytes 2359300
  378.7 11.5 all-to-all-start.3
  391.1 24.4 %copy-start.11 = (f32[512,768]{1,0:T(8,128)}, f32[512,768]{1,0:T(8,128)S(1)}, u32[]{:S(2)}) copy-start(f32[512,768]{1,0:T(8,128)S(1)} %get-tuple-element.374) | copy-start | bytes 4718596
  391.1 24.4 %copy-start.25 = (f32[512]{0:T(512)}, f32[512]{0:T(512)S(1)}, u32[]{:S(2)}) copy-start(f32[512]{0:T(512)S(1)} %broadcast_multiply_fusion.5) | copy-start | bytes 6148
  391.5 24.1 %copy-start.35 = (f32[512]{0:T(512)}, f32[512]{0:T(512)S(1)}, u32[]{:S(2)}) copy-start(f32[512]{0:T(512)S(1)} %add_rsqrt_fusion.1) | copy-start | bytes 6148
  397.0 14.7 slice-start.2
  400.9 10.7 copy-start.10
  416.0 19.3 %copy-start.4 = (f32[512,768]{1,0:T(8,128)}, f32[512,768]{1,0:T(8,128)S(1)}, u32[]{:S(2)}) copy-start(f32[512,768]{1,0:T(8,128)S(1)} %subtract_multiply_fusion) | copy-start | bytes 4718596
  420.1 17.5 %all-to-all-start.4 = ((bf16[512,2,384]{0,2,1:T(8,128)(2,1)}), bf16[512,2,384]{0,2,1:T(8,128)(2,1)S(1)}, u32[]{:S(2)}, u32[]{:S(2)}) async-start(bf16[512,2,384]{0,2,1:T(8,128)(2,1)} %bitcast.289), calls=%async_computation.4 | async-start | bytes 1572864 | tf_op jit(solution)/shard_map/all_to_all | solution.py:205
  423.6 687.3 %reduce-scatter.13.cloned.1.call-start = ((), (), s32[]{:S(2)}) async-start(), calls=%async_computation.14 | async-start | bytes 2506752 | tf_op jit(solution)/shard_map/reduce_scatter | solution.py:289
  437.5 674.9 %reduce-scatter.23.cloned.1.call-start = ((), (), s32[]{:S(2)}) async-start(), calls=%async_computation.19 | async-start | bytes 2506752
  542.3 22.0 %copy-start.3 = (bf16[16,64,6,64]{1,0,3,2:T(8,128)(2,1)S(1)}, bf16[16,64,6,64]{1,0,3,2:T(8,128)(2,1)}, u32[]{:S(2)}) copy-start(bf16[16,64,6,64]{1,0,3,2:T(8,128)(2,1)} %reshape.690) | copy-start | bytes 2359300
  649.1 12.9 copy-start.62
  733.9 36.4 %collective-permute-start.2 = (bf16[1024,768]{1,0:T(8,128)(2,1)}, bf16[1024,768]{1,0:T(8,128)(2,1)}, u32[]{:S(2)}, u32[]{:S(2)}) collective-permute-start(bf16[1024,768]{1,0:T(8,128)(2,1)} %get-tuple-element.436), channel_id=1, source_target_pairs={{2,0},{4,2},{6,4},{8,6},{10,8},{12,10},{14,12},{16,14},{18,16},{20... | collective-permute-start | bytes 4718600 | tf_op jit(solution)/shard_map/while/body/eval_jaxpr/ppermute | solution.py:16
  735.2 38.5 %collective-permute-start.3 = (bf16[1024,768]{1,0:T(8,128)(2,1)S(1)}, bf16[1024,768]{1,0:T(8,128)(2,1)}, u32[]{:S(2)}, u32[]{:S(2)}) collective-permute-start(bf16[1024,768]{1,0:T(8,128)(2,1)S(1)} %get-tuple-element.437), channel_id=1, source_target_pairs={{0,2},{2,4},{4,6},{6,8},{8,10},{10,12},{12,14},{14,16},{16,18},{18... | collective-permute-start | bytes 4718600 | tf_op jit(solution)/shard_map/while/body/eval_jaxpr/ppermute | solution.py:16
  783.6 37.8 %collective-permute-start.2 = (bf16[1024,768]{1,0:T(8,128)(2,1)}, bf16[1024,768]{1,0:T(8,128)(2,1)}, u32[]{:S(2)}, u32[]{:S(2)}) collective-permute-start(bf16[1024,768]{1,0:T(8,128)(2,1)} %get-tuple-element.436), channel_id=1, source_target_pairs={{2,0},{4,2},{6,4},{8,6},{10,8},{12,10},{14,12},{16,14},{18,16},{20... | collective-permute-start | bytes 4718600 | tf_op jit(solution)/shard_map/while/body/eval_jaxpr/ppermute | solution.py:16
  784.9 39.8 %collective-permute-start.3 = (bf16[1024,768]{1,0:T(8,128)(2,1)S(1)}, bf16[1024,768]{1,0:T(8,128)(2,1)}, u32[]{:S(2)}, u32[]{:S(2)}) collective-permute-start(bf16[1024,768]{1,0:T(8,128)(2,1)S(1)} %get-tuple-element.437), channel_id=1, source_target_pairs={{0,2},{2,4},{4,6},{6,8},{8,10},{10,12},{12,14},{14,16},{16,18},{18... | collective-permute-start | bytes 4718600 | tf_op jit(solution)/shard_map/while/body/eval_jaxpr/ppermute | solution.py:16
  834.7 23.0 %collective-permute-start.2 = (bf16[1024,768]{1,0:T(8,128)(2,1)}, bf16[1024,768]{1,0:T(8,128)(2,1)}, u32[]{:S(2)}, u32[]{:S(2)}) collective-permute-start(bf16[1024,768]{1,0:T(8,128)(2,1)} %get-tuple-element.436), channel_id=1, source_target_pairs={{2,0},{4,2},{6,4},{8,6},{10,8},{12,10},{14,12},{16,14},{18,16},{20... | collective-permute-start | bytes 4718600 | tf_op jit(solution)/shard_map/while/body/eval_jaxpr/ppermute | solution.py:16
  836.0 25.1 %collective-permute-start.3 = (bf16[1024,768]{1,0:T(8,128)(2,1)S(1)}, bf16[1024,768]{1,0:T(8,128)(2,1)}, u32[]{:S(2)}, u32[]{:S(2)}) collective-permute-start(bf16[1024,768]{1,0:T(8,128)(2,1)S(1)} %get-tuple-element.437), channel_id=1, source_target_pairs={{0,2},{2,4},{4,6},{6,8},{8,10},{10,12},{12,14},{14,16},{16,18},{18... | collective-permute-start | bytes 4718600 | tf_op jit(solution)/shard_map/while/body/eval_jaxpr/ppermute | solution.py:16
  871.1 35.6 %collective-permute-start.2 = (bf16[1024,768]{1,0:T(8,128)(2,1)}, bf16[1024,768]{1,0:T(8,128)(2,1)}, u32[]{:S(2)}, u32[]{:S(2)}) collective-permute-start(bf16[1024,768]{1,0:T(8,128)(2,1)} %get-tuple-element.436), channel_id=1, source_target_pairs={{2,0},{4,2},{6,4},{8,6},{10,8},{12,10},{14,12},{16,14},{18,16},{20... | collective-permute-start | bytes 4718600 | tf_op jit(solution)/shard_map/while/body/eval_jaxpr/ppermute | solution.py:16
  872.4 37.6 %collective-permute-start.3 = (bf16[1024,768]{1,0:T(8,128)(2,1)S(1)}, bf16[1024,768]{1,0:T(8,128)(2,1)}, u32[]{:S(2)}, u32[]{:S(2)}) collective-permute-start(bf16[1024,768]{1,0:T(8,128)(2,1)S(1)} %get-tuple-element.437), channel_id=1, source_target_pairs={{0,2},{2,4},{4,6},{6,8},{8,10},{10,12},{12,14},{14,16},{16,18},{18... | collective-permute-start | bytes 4718600 | tf_op jit(solution)/shard_map/while/body/eval_jaxpr/ppermute | solution.py:16
  917.5 13.5 copy-start.8
  934.9 181.9 %reduce-scatter.21.cloned.1.call-start = ((), (), s32[]{:S(2)}) async-start(), calls=%async_computation.18 | async-start | bytes 2506752
  955.2 276.5 %reduce-scatter.17.cloned.1.call-start = ((), (), s32[]{:S(2)}) async-start(), calls=%async_computation.16 | async-start | bytes 10027008 | tf_op jit(solution)/shard_map/reduce_scatter | solution.py:293
  966.2 380.6 %reduce-scatter.15.cloned.1.call-start = ((), (), s32[]{:S(2)}) async-start(), calls=%async_computation.15 | async-start | bytes 10027008 | tf_op jit(solution)/shard_map/reduce_scatter | solution.py:292
  974.8 438.8 %reduce-scatter.19.cloned.1.call-start = ((), (), s32[]{:S(2)}) async-start(), calls=%async_computation.17 | async-start | bytes 2506752 | tf_op jit(solution)/shard_map/reduce_scatter | solution.py:286
  1001.6 347.0 %copy-start.17 = (bf16[2,512,384]{1,2,0:T(8,128)(2,1)S(1)}, bf16[2,512,384]{1,2,0:T(8,128)(2,1)}, u32[]{:S(2)}) copy-start(bf16[2,512,384]{1,2,0:T(8,128)(2,1)} %copy-done.16) | copy-start | bytes 2359300
  1001.6 347.0 %copy-start.63 = (bf16[768,768]{1,0:T(8,128)(2,1)S(1)}, bf16[768,768]{1,0:T(8,128)(2,1)}, u32[]{:S(2)}) copy-start(bf16[768,768]{1,0:T(8,128)(2,1)} %param.20) | copy-start | bytes 3538948
  1001.7 455.7 %all-reduce.10.cloned.1.call-start = ((), (), s32[]{:S(2)}) async-start(), calls=%async_computation.20 | async-start | bytes 2113536 | tf_op jit(solution)/shard_map/psum | solution.py:299
  1118.5 231.0 %copy-start.15 = (bf16[512,2,384]{0,2,1:T(8,128)(2,1)S(1)}, bf16[512,2,384]{0,2,1:T(8,128)(2,1)}, u32[]{:S(2)}) copy-start(bf16[512,2,384]{0,2,1:T(8,128)(2,1)} %copy.239) | copy-start | bytes 2359300
  1351.8 114.1 %copy-start.1 = (bf16[768,768]{1,0:T(8,128)(2,1)S(1)}, bf16[768,768]{1,0:T(8,128)(2,1)}, u32[]{:S(2)}) copy-start(bf16[768,768]{1,0:T(8,128)(2,1)} %param.23) | copy-start | bytes 3538948
  (55 other events, 276.6 us)
Sparse Core Ops, SparseCore 0:
  437.7 116.0 reduce-scatter.12
  935.0 115.9 reduce-scatter.22
  1054.7 62.0 reduce-scatter.20
  1121.3 110.3 reduce-scatter.16
  1235.6 111.0 reduce-scatter.14
  1350.9 62.7 reduce-scatter.18
  1417.4 39.9 all-reduce.9
